TPU v7x, 32 devices: a whole 2x2x4 slice. The times are simulated.
32 devices in a mesh: seq: 2 (over y), fsdp: 16 (over z, x, core).
Axes of the slice: x: 2, y: 2, z: 4, core: 2. Of those that a mesh axis runs over, the one named last changes fastest.
Arguments:
- tokens: bfloat16 [16, 1024, 1024], P('fsdp', 'seq'), may hold values from -6 to 6
- blocks: int32 [16, 1024], P('fsdp'), may hold values from 0 to 7, never falling along the last dimension, each value on 1 to 256 neighbouring positions
- first_gain: bfloat16 [1024], P('fsdp'), may hold values from 0.5 to 1.5
- first_shift: bfloat16 [1024], P('fsdp'), may hold values from -1.5 to 1.5
- joint_weight: bfloat16 [1024, 3072], P('fsdp'), may hold values from -0.1875 to 0.1875
- joint_bias: bfloat16 [2, 1024], P(None, 'fsdp'), may hold values from -1.5 to 1.5
- output_weight: bfloat16 [1024, 1024], P('fsdp'), may hold values from -0.75 to 0.75
- output_bias: bfloat16 [1024], P('fsdp'), may hold values from -1.5 to 1.5
- second_gain: bfloat16 [1024], P('fsdp'), may hold values from 0.5 to 1.5
- second_shift: bfloat16 [1024], P('fsdp'), may hold values from -1.5 to 1.5
- upward_weight: bfloat16 [1024, 4096], P('fsdp'), may hold values from -0.1875 to 0.1875
- upward_bias: bfloat16 [4096], P('fsdp'), may hold values from -1.5 to 1.5
- downward_weight: bfloat16 [4096, 1024], P('fsdp'), may hold values from -0.125 to 0.125
- downward_bias: bfloat16 [1024], P('fsdp'), may hold values from -1.5 to 1.5
- cotangent: bfloat16 [16, 1024, 1024], P('fsdp', 'seq'), may hold values from -6 to 6
Outputs:
- result: bfloat16 [16, 1024, 1024], P('fsdp', 'seq')
- grad_tokens: float32 [16, 1024, 1024], P('fsdp', 'seq')
- grad_first_gain: float32 [1024], P('fsdp')
- grad_first_shift: float32 [1024], P('fsdp')
- grad_joint_weight: float32 [1024, 3072], P('fsdp')
- grad_joint_bias: float32 [2, 1024], P(None, 'fsdp')
- grad_output_weight: float32 [1024, 1024], P('fsdp')
- grad_output_bias: float32 [1024], P('fsdp')
- grad_second_gain: float32 [1024], P('fsdp')
- grad_second_shift: float32 [1024], P('fsdp')
- grad_upward_weight: float32 [1024, 4096], P('fsdp')
- grad_upward_bias: float32 [4096], P('fsdp')
- grad_downward_weight: float32 [4096, 1024], P('fsdp')
- grad_downward_bias: float32 [1024], P('fsdp')
Inputs may be any that keep to these rules, and one draw needn't show every extreme that they name: `blocks`: along each sequence the block number never falls; every block has 1 to 256 tokens, and one has exactly 256.
All inputs are finite; a program needn't handle non-finite values.
Results may differ from a plain program's by a relative error of at most 0.014.
Values may be sent and summed in bfloat16 or wider, within the bound.
No kernel may reach another device: no remote copies, remote signals or barrier semaphores. Data moves between devices by JAX's collectives and lax.ppermute only.
A program may use at most 192 MiB of HBM per device.

v0:
```python
import jax
import jax.numpy as jnp
from jax import lax
from jax.sharding import PartitionSpec as P

HEADS = 16
HEAD_DIM = 64


EPSILON = 1e-05


def scaled_norm(values, gain):
    center = values - jnp.mean(values, axis=-1, keepdims=True)
    spread = jnp.mean(center * center, axis=-1, keepdims=True)
    return center * lax.rsqrt(spread + EPSILON) * gain


def gelu_tanh(values):
    return jax.nn.gelu(values, approximate=True)


def matmul(left, right):
    return jnp.dot(left, right, preferred_element_type=jnp.float32)


def left_contract(left, right):
    return lax.dot_general(
        left, right, (((0,), (0,)), ((), ())), preferred_element_type=jnp.float32
    )


def right_contract(left, right):
    return lax.dot_general(
        left, right, (((1,), (1,)), ((), ())), preferred_element_type=jnp.float32
    )


def masked_scores(queries, keys_in, slope, distance, allowed):
    scores = right_contract(queries, keys_in) * HEAD_DIM ** (-0.5) - slope * distance
    return jnp.where(allowed, scores, -1e30)


def attend_heads(heads, slopes, distance, allowed):

    def one_head(packed):
        queries, keys_in, values_in, slope = packed
        scores = masked_scores(queries, keys_in, slope, distance, allowed)
        top_score = jnp.max(scores, axis=1, keepdims=True)
        totals = jnp.sum(jnp.exp(scores - top_score), axis=1, keepdims=True)
        log_total = top_score + jnp.log(totals)
        probs = jnp.exp(scores - log_total).astype(jnp.bfloat16)
        return (matmul(probs, values_in).astype(jnp.bfloat16), log_total[:, 0])

    return lax.map(one_head, (heads[0], heads[1], heads[2], slopes))


def attend_back(heads, log_totals, grad_heads, slopes, distance, allowed):

    def one_head(packed):
        queries, keys_in, values_in, log_total, grad_head, slope = packed
        scores = masked_scores(queries, keys_in, slope, distance, allowed)
        probs = jnp.exp(scores - log_total[:, None])
        grad_probs = right_contract(grad_head, values_in)
        inner = jnp.sum(probs * grad_probs, axis=1, keepdims=True)
        grad_scores = (probs * (grad_probs - inner)).astype(jnp.bfloat16)
        factor = HEAD_DIM ** (-0.5)
        grad_queries = matmul(grad_scores, keys_in) * factor
        grad_keys = left_contract(grad_scores, queries) * factor
        grad_values = left_contract(probs.astype(jnp.bfloat16), grad_head)
        return jnp.stack([grad_queries, grad_keys, grad_values]).astype(jnp.bfloat16)

    return lax.map(one_head, (heads[0], heads[1], heads[2], log_totals, grad_heads, slopes))


def per_device(
    tokens,
    blocks,
    first_gain,
    first_shift,
    joint_weight,
    joint_bias,
    output_weight,
    output_bias,
    second_gain,
    second_shift,
    upward_weight,
    upward_bias,
    downward_weight,
    downward_bias,
    cotangent,
):
    groups = lax.axis_size("seq")
    token_count = tokens.shape[1]
    model_width = tokens.shape[2]
    seq_length = token_count * groups
    local_heads = HEADS // groups
    group_width = model_width // groups
    inputs = tokens[0].astype(jnp.float32)
    attn_set = (
        lax.all_gather(first_gain, "fsdp", axis=0, tiled=True),
        lax.all_gather(first_shift, "fsdp", axis=0, tiled=True),
        lax.all_gather(joint_weight, "fsdp", axis=0, tiled=True),
        lax.all_gather(joint_bias, "fsdp", axis=1, tiled=True),
        lax.all_gather(output_weight, "fsdp", axis=0, tiled=True),
        lax.all_gather(output_bias, "fsdp", axis=0, tiled=True),
    )
    normed_one = (
        scaled_norm(inputs, attn_set[0].astype(jnp.float32)) + attn_set[1].astype(jnp.float32)
    ).astype(jnp.bfloat16)
    bias_full = jnp.concatenate(
        [attn_set[3][0], jnp.zeros((model_width,), jnp.bfloat16), attn_set[3][1]]
    ).astype(jnp.float32)
    joint = (matmul(normed_one, attn_set[2]) + bias_full).astype(jnp.bfloat16)
    joint = joint.reshape(token_count, 3, groups, group_width)
    heads = lax.all_to_all(joint, "seq", split_axis=2, concat_axis=0, tiled=True)
    heads = heads.reshape(seq_length, 3, local_heads, HEAD_DIM).transpose(1, 2, 0, 3)
    positions = jnp.arange(seq_length)
    distance = jnp.abs(positions[:, None] - positions[None, :]).astype(jnp.float32)
    block_row = blocks[0]
    allowed = block_row[None, :] <= block_row[:, None]
    head_index = lax.axis_index("seq") * local_heads + jnp.arange(local_heads)
    slopes = jnp.exp2(-8.0 * (head_index.astype(jnp.float32) + 1.0) / HEADS)
    attended, log_totals = attend_heads(heads, slopes, distance, allowed)
    flat_heads = attended.transpose(1, 0, 2).reshape(seq_length, 1, group_width)
    mixed = lax.all_to_all(flat_heads, "seq", split_axis=0, concat_axis=1, tiled=True).reshape(
        token_count, model_width
    )
    hidden = inputs + matmul(mixed, attn_set[4]) + attn_set[5].astype(jnp.float32)
    mlp_set = (
        lax.all_gather(second_gain, "fsdp", axis=0, tiled=True),
        lax.all_gather(second_shift, "fsdp", axis=0, tiled=True),
        lax.all_gather(upward_weight, "fsdp", axis=0, tiled=True),
        lax.all_gather(upward_bias, "fsdp", axis=0, tiled=True),
        lax.all_gather(downward_weight, "fsdp", axis=0, tiled=True),
        lax.all_gather(downward_bias, "fsdp", axis=0, tiled=True),
    )
    normed_two = (
        scaled_norm(hidden, mlp_set[0].astype(jnp.float32)) + mlp_set[1].astype(jnp.float32)
    ).astype(jnp.bfloat16)
    upward = matmul(normed_two, mlp_set[2]) + mlp_set[3].astype(jnp.float32)
    activated = gelu_tanh(upward).astype(jnp.bfloat16)
    output = hidden + matmul(activated, mlp_set[4]) + mlp_set[5].astype(jnp.float32)
    back_gain_two, back_upward, back_downward = (
        lax.all_gather(second_gain, "fsdp", axis=0, tiled=True),
        lax.all_gather(upward_weight, "fsdp", axis=0, tiled=True),
        lax.all_gather(downward_weight, "fsdp", axis=0, tiled=True),
    )
    grad_output = cotangent[0].astype(jnp.float32)
    grad_low = grad_output.astype(jnp.bfloat16)
    grad_down_bias = jnp.sum(grad_low.astype(jnp.float32), axis=0)
    grad_down_weight = left_contract(activated, grad_low)
    grad_act = right_contract(grad_low, back_downward)
    gelu_back = jax.vjp(gelu_tanh, upward)[1]
    grad_up = gelu_back(grad_act)[0].astype(jnp.bfloat16)
    grad_up_bias = jnp.sum(grad_up.astype(jnp.float32), axis=0)
    grad_up_weight = left_contract(normed_two, grad_up)
    grad_normed_two = right_contract(grad_up, back_upward)
    norm_two_back = jax.vjp(scaled_norm, hidden, back_gain_two.astype(jnp.float32))[1]
    grad_hidden_norm, grad_gain_two = norm_two_back(grad_normed_two)
    grad_shift_two = jnp.sum(grad_normed_two, axis=0)
    grad_hidden = grad_output + grad_hidden_norm
    back_gain_one, back_joint, back_output = (
        lax.all_gather(first_gain, "fsdp", axis=0, tiled=True),
        lax.all_gather(joint_weight, "fsdp", axis=0, tiled=True),
        lax.all_gather(output_weight, "fsdp", axis=0, tiled=True),
    )
    hidden_low = grad_hidden.astype(jnp.bfloat16)
    grad_out_bias = jnp.sum(hidden_low.astype(jnp.float32), axis=0)
    grad_out_weight = left_contract(mixed, hidden_low)
    grad_mixed = right_contract(hidden_low, back_output).astype(jnp.bfloat16)
    grad_mixed = grad_mixed.reshape(token_count, groups, group_width)
    grad_heads = lax.all_to_all(grad_mixed, "seq", split_axis=1, concat_axis=0, tiled=True)
    grad_heads = grad_heads.reshape(seq_length, local_heads, HEAD_DIM).transpose(1, 0, 2)
    grad_stack = attend_back(heads, log_totals, grad_heads, slopes, distance, allowed)
    grad_stack = grad_stack.transpose(2, 1, 0, 3).reshape(seq_length, 3, 1, group_width)
    grad_joint = lax.all_to_all(grad_stack, "seq", split_axis=0, concat_axis=2, tiled=True)
    grad_joint = grad_joint.reshape(token_count, 3 * model_width)
    joint_sums = jnp.sum(grad_joint.astype(jnp.float32), axis=0)
    grad_joint_bias = jnp.stack([joint_sums[:model_width], joint_sums[2 * model_width :]])
    grad_joint_weight = left_contract(normed_one, grad_joint)
    grad_normed_one = right_contract(grad_joint, back_joint)
    norm_one_back = jax.vjp(scaled_norm, inputs, back_gain_one.astype(jnp.float32))[1]
    grad_input_norm, grad_gain_one = norm_one_back(grad_normed_one)
    grad_shift_one = jnp.sum(grad_normed_one, axis=0)
    grad_inputs = grad_hidden + grad_input_norm
    every_sum = (
        lax.psum_scatter(grad_gain_one, "fsdp", scatter_dimension=0, tiled=True),
        lax.psum_scatter(grad_shift_one, "fsdp", scatter_dimension=0, tiled=True),
        lax.psum_scatter(grad_joint_weight, "fsdp", scatter_dimension=0, tiled=True),
        lax.psum_scatter(grad_joint_bias, "fsdp", scatter_dimension=1, tiled=True),
        lax.psum_scatter(grad_out_weight, "fsdp", scatter_dimension=0, tiled=True),
        lax.psum_scatter(grad_out_bias, "fsdp", scatter_dimension=0, tiled=True),
        lax.psum_scatter(grad_gain_two, "fsdp", scatter_dimension=0, tiled=True),
        lax.psum_scatter(grad_shift_two, "fsdp", scatter_dimension=0, tiled=True),
        lax.psum_scatter(grad_up_weight, "fsdp", scatter_dimension=0, tiled=True),
        lax.psum_scatter(grad_up_bias, "fsdp", scatter_dimension=0, tiled=True),
        lax.psum_scatter(grad_down_weight, "fsdp", scatter_dimension=0, tiled=True),
        lax.psum_scatter(grad_down_bias, "fsdp", scatter_dimension=0, tiled=True),
    )
    attn_sums = every_sum[:6]
    mlp_sums = every_sum[6:]
    totals = (
        lax.psum(attn_sums[0].astype(jnp.bfloat16), "seq").astype(jnp.float32),
        lax.psum(attn_sums[1].astype(jnp.bfloat16), "seq").astype(jnp.float32),
        lax.psum(attn_sums[2].astype(jnp.bfloat16), "seq").astype(jnp.float32),
        lax.psum(attn_sums[3].astype(jnp.bfloat16), "seq").astype(jnp.float32),
        lax.psum(attn_sums[4].astype(jnp.bfloat16), "seq").astype(jnp.float32),
        lax.psum(attn_sums[5].astype(jnp.bfloat16), "seq").astype(jnp.float32),
        lax.psum(mlp_sums[0].astype(jnp.bfloat16), "seq").astype(jnp.float32),
        lax.psum(mlp_sums[1].astype(jnp.bfloat16), "seq").astype(jnp.float32),
        lax.psum(mlp_sums[2].astype(jnp.bfloat16), "seq").astype(jnp.float32),
        lax.psum(mlp_sums[3].astype(jnp.bfloat16), "seq").astype(jnp.float32),
        lax.psum(mlp_sums[4].astype(jnp.bfloat16), "seq").astype(jnp.float32),
        lax.psum(mlp_sums[5].astype(jnp.bfloat16), "seq").astype(jnp.float32),
    )
    return (
        output.astype(jnp.bfloat16)[None],
        grad_inputs[None],
        totals[0],
        totals[1],
        totals[2],
        totals[3],
        totals[4],
        totals[5],
        totals[6],
        totals[7],
        totals[8],
        totals[9],
        totals[10],
        totals[11],
    )


def solution(mesh):
    in_specs = (
        P("fsdp", "seq", None),
        P("fsdp", None),
        P("fsdp"),
        P("fsdp"),
        P("fsdp", None),
        P(None, "fsdp"),
        P("fsdp", None),
        P("fsdp"),
        P("fsdp"),
        P("fsdp"),
        P("fsdp", None),
        P("fsdp"),
        P("fsdp", None),
        P("fsdp"),
        P("fsdp", "seq", None),
    )
    out_specs = (
        P("fsdp", "seq", None),
        P("fsdp", "seq", None),
        P("fsdp"),
        P("fsdp"),
        P("fsdp", None),
        P(None, "fsdp"),
        P("fsdp", None),
        P("fsdp"),
        P("fsdp"),
        P("fsdp"),
        P("fsdp", None),
        P("fsdp"),
        P("fsdp", None),
        P("fsdp"),
    )
    return jax.shard_map(
        per_device, mesh=mesh, in_specs=in_specs, out_specs=out_specs, check_vma=False
    )
```

profile of v0, /device:TPU:0, one launch (start us, length us, event | category | flops | bytes accessed | tf_op | source)
XLA Modules:
  0.0 1121.6 jit_solution(8430259839319301549)
XLA Ops:
  10.1 23.6 %all-gather = bf16[16,64,2]{1,2,0:T(2,128)(2,1)S(1)} all-gather(bf16[1,64,2]{1,2,0:T(2,128)(2,1)} %bitcast.245), channel_id=1, replica_groups=mesh['seq'=2,'fsdp'=16] {'fsdp'}, dimensions={0}, use_global_device_ids=true | all-gather | bytes 4352 | tf_op jit(solution)/shard_map/all_gather | solution.py:104
  38.8 59.6 %all-reduce.14 = (bf16[1024]{0:T(1024)(128)(2,1)S(1)}, bf16[1024]{0:T(1024)(128)(2,1)S(1)}, bf16[1024]{0:T(1024)(128)(2,1)S(1)}, bf16[1024]{0:T(1024)(128)(2,1)}...) all-reduce(bf16[1024]{0:T(1024)(128)(2,1)S(1)} %dynamic-update-slic, ...), channel_id=1, replica_groups=mesh['seq'=2,'fsdp'=16] {'fsdp'}, use_global_device_ids=true, to_apply=%add.1 | all-reduce | flops 6144 | bytes 24576
  98.5 8.1 add_convert_fusion
  106.7 8.3 reshape.247
  115.0 8.6 copy.73
  129.2 31.7 %all-to-all-done = bf16[512,3,2,512]{0,3,1,2:T(8,128)(2,1)} async-done(((bf16[512,3,2,512]{0,3,1,2:T(8,128)(2,1)}), bf16[512,3,2,512]{0,3,1,2:T(8,128)(2,1)}, u32[]{:S(2)}, u32[]{:S(2)}) %all-to-all-start) | async-done | bytes 3145760 | tf_op jit(solution)/shard_map/all_to_all | solution.py:116
  182.7 47.9 %while.24 = (s32[]{:T(128)}, bf16[8,1024,64]{1,2,0:T(8,128)(2,1)}, f32[8,1024]{1,0:T(8,128)S(1)}, bf16[8,1024,64]{2,1,0:T(8,128)(2,1)}, bf16[8,1024,64]{2,1,0:T(...) while((s32[]{:T(128)}, bf16[8,1024,64]{1,2,0:T(8,128)(2,1)}, ...), condition=%wide.region_5.6_spmd.clone, body=%wide.region_2.5_spmd.clone.sunk | while | flops 282131456 | bytes 13548157 | solution.py:55
  244.0 19.0 %all-gather.1 = bf16[16,1,256]{2,1,0:T(2,128)(2,1)S(1)} all-gather(bf16[1,1,256]{2,1,0:T(2,128)(2,1)S(1)} %reshape.275), channel_id=1, replica_groups=mesh['seq'=2,'fsdp'=16] {'fsdp'}, dimensions={0}, use_global_device_ids=true | all-gather | bytes 8704 | tf_op jit(solution)/shard_map/all_gather | solution.py:134
  272.3 10.6 fusion.109
  282.9 14.3 %convert_reduce_fusion = (f32[4096]{0:T(1024)}, bf16[512,4096]{1,0:T(8,128)(2,1)S(1)}) fusion(f32[512,4096]{1,0:T(8,128)} %fusion.109, f32[4096]{0:T(1024)S(1)} %bitcast.240, bf16[4096,1024]{1,0:T(8,128)(2,1)} %all-gather.13.cloned.1.call-done, bf16[1,512,1024]{2,1,0:T(8,128)(2,1)S(1)} %copy-done.6), kind=kOutput, calls=%fused_computation.72 | convolution fusion | flops 4343197696 | bytes 22052864 | tf_op jit(solution)/shard_map/dot_general | solution.py:34
  315.0 10.9 all-to-all-done.2
  327.9 99.5 %while.25 = (s32[]{:T(128)}, bf16[8,3,1024,64]{2,3,0,1:T(8,128)(2,1)}, bf16[8,1024,64]{2,1,0:T(8,128)(2,1)}, bf16[8,1024,64]{2,1,0:T(8,128)(2,1)}, f32[8]{0:T(12...) while((s32[]{:T(128)}, ...), condition=%wide.region_12.13_spmd.clone, body=%wide.region_10.12_spmd.clone.sunk | while | flops 688323584 | bytes 34241164 | solution.py:73
  427.3 7.6 copy.87
  434.9 51.4 %all_to_all.60 = bf16[1024,3,1,512]{3,1,2,0:T(4,128)(2,1)S(1)} all-to-all(bf16[1024,3,1,512]{3,1,2,0:T(4,128)(2,1)} %copy.87), channel_id=1, replica_groups=mesh['seq'=2,'fsdp'=16] {'seq'}, dimensions={0} | all-to-all | bytes 6291456 | tf_op jit(solution)/shard_map/all_to_all | solution.py:177
  490.0 10.5 fusion.88
  500.8 16.2 %fusion.108 = f32[1024,4096]{1,0:T(8,128)} fusion(bf16[512,4096]{1,0:T(8,128)(2,1)} %copy-done.33, f32[512,1024]{1,0:T(8,128)} %copy-done.4, f32[1024]{0:T(1024)S(1)} %convert_element_type.192, f32[1024]{0:T(1024)S(1)} %convert_element_type.191, f32[512]{0:T(512)S(1)} %fusion.106, f32[512]{0:T(512)S(1)} %broadcast_multiply_fusion), kind=kOutput, calls=%fused_computation.153 | convolution fusion | flops 4297588736 | bytes 23080960 | tf_op jit(solution)/shard_map/dot_general | solution.py:28
  517.1 17.9 %fusion.91 = f32[4096,1024]{1,0:T(8,128)} fusion(bf16[1,512,1024]{2,1,0:T(8,128)(2,1)} %param.33, f32[512,4096]{1,0:T(8,128)} %fusion.109, f32[4096]{0:T(1024)S(1)} %bitcast.241), kind=kOutput, calls=%fused_computation.116 | convolution fusion | flops 4315938816 | bytes 26230784 | tf_op jit(solution)/shard_map/dot_general | solution.py:28
  538.8 12.9 %fusion.85 = bf16[1,512,1024]{2,1,0:T(8,128)(2,1)} fusion(f32[512,1024]{1,0:T(8,128)} %copy-done.4, bf16[4096,1024]{1,0:T(8,128)(2,1)} %all-gather.13.cloned.1.call-done, f32[1024]{0:T(1024)S(1)} %convert_element_type.196, f32[512,4096]{1,0:T(8,128)} %fusion.109, f32[4096]{0:T(1024)S(1)} %bitcast.242), kind=kOutput, calls=%fused_computation.109 | convolution fusion | flops 4317511680 | bytes 19943424 | tf_op jit(solution)/shard_map/dot_general | solution.py:24
  553.4 79.2 %reduce-scatter.8.cloned.1.call-done = f32[64,3072]{1,0:T(8,128)} async-done(((f32[1024,3072]{1,0:T(8,128)}), f32[64,3072]{1,0:T(8,128)}) %reduce-scatter.8.cloned.1.call-update) | async-done | bytes 786448 | tf_op jit(solution)/shard_map/reduce_scatter | solution.py:190
  634.5 178.8 %reduce-scatter.12.cloned.1.call-done = f32[64,4096]{1,0:T(8,128)} async-done(((f32[1024,4096]{1,0:T(8,128)}), f32[64,4096]{1,0:T(8,128)}) %reduce-scatter.12.cloned.1.call-update) | async-done | bytes 1048592 | tf_op jit(solution)/shard_map/reduce_scatter | solution.py:196
  815.4 178.5 %reduce-scatter.14.cloned.1.call-done = f32[256,1024]{1,0:T(8,128)} async-done(((f32[4096,1024]{1,0:T(8,128)}), f32[256,1024]{1,0:T(8,128)}) %reduce-scatter.14.cloned.1.call-update) | async-done | bytes 1048592 | tf_op jit(solution)/shard_map/reduce_scatter | solution.py:198
  996.1 6.9 fusion.110
  1007.0 59.6 %all-reduce.13 = (bf16[1024]{0:T(1024)(128)(2,1)S(1)}, bf16[1024]{0:T(1024)(128)(2,1)S(1)}, bf16[1024]{0:T(1024)(128)(2,1)S(1)}, bf16[1024]{0:T(1024)(128)(2,1)S...) all-reduce(f32[1024]{0:T(1024)S(1)} %get-tuple-element.229, ...), channel_id=2, replica_groups=mesh['seq'=2,'fsdp'=16] {'fsdp'}, use_global_device_ids=true, to_apply=%region_16.17.clone | all-reduce | flops 10240 | bytes 61440
  1077.3 30.3 %all-reduce.19.cloned.1.call-done = (bf16[64,3072]{1,0:T(8,128)(2,1)}, bf16[64,1024]{1,0:T(8,128)(2,1)}, bf16[64,4096]{1,0:T(8,128)(2,1)}, bf16[256,1024]{1,0:T(8,128)(2,1)}) async-done(((bf16[64,3072]{1,0:T(8,128)(2,1)}, bf16[64,1024]{1,0:T(8,128)(2,1)}, bf16[64,4096]{1,0:T(8,128)(2,1)}, bf16[256,1024]{1,0:T(8,128)(2,1)}), (bf16[64,3072]{1,0:T(8,128)(2,1)}, bf16[64,1024]{1,0:T(8,128)(2,1)}, ...) | async-done | bytes 1572880 | tf_op jit(solution)/shard_map/psum | solution.py:206
  (316 shorter events, 259.5 us)
Async XLA Ops:
  7.2 29.0 %copy-start.23 = (u32[32]{0:T(128)S(1)}, u32[32]{0:T(128)}, u32[]{:S(2)}) copy-start(u32[32]{0:T(128)} %constant.97) | copy-start | bytes 388
  7.2 30.2 %copy-start.26 = (bf16[64]{0:T(256)(128)(2,1)S(1)}, bf16[64]{0:T(256)(128)(2,1)}, u32[]{:S(2)}) copy-start(bf16[64]{0:T(256)(128)(2,1)} %param.22) | copy-start | bytes 388
  7.2 30.5 %copy-start.27 = (bf16[64]{0:T(256)(128)(2,1)S(1)}, bf16[64]{0:T(256)(128)(2,1)}, u32[]{:S(2)}) copy-start(bf16[64]{0:T(256)(128)(2,1)} %param.21) | copy-start | bytes 388
  7.2 30.7 %copy-start.28 = (bf16[64]{0:T(256)(128)(2,1)S(1)}, bf16[64]{0:T(256)(128)(2,1)}, u32[]{:S(2)}) copy-start(bf16[64]{0:T(256)(128)(2,1)} %param.26) | copy-start | bytes 388
  7.2 30.9 %copy-start.29 = (bf16[64]{0:T(256)(128)(2,1)S(1)}, bf16[64]{0:T(256)(128)(2,1)}, u32[]{:S(2)}) copy-start(bf16[64]{0:T(256)(128)(2,1)} %param.32) | copy-start | bytes 388
  7.2 31.1 %copy-start.30 = (bf16[64]{0:T(256)(128)(2,1)S(1)}, bf16[64]{0:T(256)(128)(2,1)}, u32[]{:S(2)}) copy-start(bf16[64]{0:T(256)(128)(2,1)} %param.28) | copy-start | bytes 388
  7.3 31.4 %copy-start.31 = (bf16[64]{0:T(256)(128)(2,1)S(1)}, bf16[64]{0:T(256)(128)(2,1)}, u32[]{:S(2)}) copy-start(bf16[64]{0:T(256)(128)(2,1)} %param.27) | copy-start | bytes 388
  7.3 91.3 %all-gather.7.cloned.1.call-start = ((), (), s32[]{:S(2)}) async-start(), calls=%async_computation.9 | async-start | bytes 6684672 | tf_op jit(solution)/shard_map/all_gather | solution.py:103
  8.0 260.6 %all-gather.9.cloned.1.call-start = ((), (), s32[]{:S(2)}) async-start(), calls=%async_computation.10 | async-start | bytes 2228224 | tf_op jit(solution)/shard_map/all_gather | solution.py:105
  8.7 263.5 %all-gather.11.cloned.1.call-start = ((), (), s32[]{:S(2)}) async-start(), calls=%async_computation.11 | async-start | bytes 8912896 | tf_op jit(solution)/shard_map/all_gather | solution.py:133
  9.5 273.4 %all-gather.13.cloned.1.call-start = ((), (), s32[]{:S(2)}) async-start(), calls=%async_computation.12 | async-start | bytes 8912896 | tf_op jit(solution)/shard_map/all_gather | solution.py:135
  35.2 71.5 %copy-start.13 = (f32[512]{0:T(512)}, f32[512]{0:T(512)S(1)}, u32[]{:S(2)}) copy-start(f32[512]{0:T(512)S(1)} %broadcast_multiply_fusion.1) | copy-start | bytes 6148
  35.6 71.1 %copy-start.15 = (f32[512]{0:T(512)}, f32[512]{0:T(512)S(1)}, u32[]{:S(2)}) copy-start(f32[512]{0:T(512)S(1)} %fusion.105) | copy-start | bytes 6148
  123.6 37.3 %all-to-all-start = ((bf16[512,3,2,512]{0,3,1,2:T(8,128)(2,1)}), bf16[512,3,2,512]{0,3,1,2:T(8,128)(2,1)}, u32[]{:S(2)}, u32[]{:S(2)}) async-start(bf16[512,3,2,512]{0,3,1,2:T(8,128)(2,1)} %copy.73), calls=%async_computation | async-start | bytes 6291456 | tf_op jit(solution)/shard_map/all_to_all | solution.py:116
  239.5 23.5 %all-to-all-start.1 = ((bf16[2,2,131072]{2,1,0:T(2,128)(2,1)}), bf16[2,2,131072]{2,1,0:T(2,128)(2,1)}, u32[]{:S(2)}, u32[]{:S(2)}) async-start(bf16[2,2,131072]{2,1,0:T(2,128)(2,1)} %reshape.301), calls=%async_computation.1 | async-start | bytes 2097152 | tf_op jit(solution)/shard_map/all_to_all | solution.py:126
  271.8 30.4 %copy-start.4 = (f32[512,1024]{1,0:T(8,128)}, f32[512,1024]{1,0:T(8,128)S(1)}, u32[]{:S(2)}) copy-start(f32[512,1024]{1,0:T(8,128)S(1)} %get-tuple-element.313) | copy-start | bytes 6291460
  307.9 17.9 %all-to-all-start.2 = ((bf16[512,2,512]{0,2,1:T(8,128)(2,1)}), bf16[512,2,512]{0,2,1:T(8,128)(2,1)S(1)}, u32[]{:S(2)}, u32[]{:S(2)}) async-start(bf16[512,2,512]{0,2,1:T(8,128)(2,1)} %bitcast.19), calls=%async_computation.2 | async-start | bytes 2097152 | tf_op jit(solution)/shard_map/all_to_all | solution.py:173
  311.5 240.2 %reduce-scatter.10.cloned.1.call-start = ((), (), s32[]{:S(2)}) async-start(), calls=%async_computation.14 | async-start | bytes 4456448 | tf_op jit(solution)/shard_map/reduce_scatter | solution.py:192
  314.9 317.7 %reduce-scatter.8.cloned.1.call-start = ((), (), s32[]{:S(2)}) async-start(), calls=%async_computation.13 | async-start | bytes 13369344 | tf_op jit(solution)/shard_map/reduce_scatter | solution.py:190
  500.5 312.8 %reduce-scatter.12.cloned.1.call-start = ((), (), s32[]{:S(2)}) async-start(), calls=%async_computation.15 | async-start | bytes 17825792 | tf_op jit(solution)/shard_map/reduce_scatter | solution.py:196
  517.0 476.9 %reduce-scatter.14.cloned.1.call-start = ((), (), s32[]{:S(2)}) async-start(), calls=%async_computation.16 | async-start | bytes 17825792 | tf_op jit(solution)/shard_map/reduce_scatter | solution.py:198
  535.0 532.1 %reduce-scatter.16.cloned.1.call-start = ((), (), s32[]{:S(2)}) async-start(), calls=%async_computation.17 | async-start | bytes 557056
  538.5 569.1 %all-reduce.19.cloned.1.call-start = ((), (), s32[]{:S(2)}) async-start(), calls=%async_computation.18 | async-start | bytes 3145728 | tf_op jit(solution)/shard_map/psum | solution.py:206
  551.7 444.4 %copy-start.1 = (bf16[1,512,1024]{2,1,0:T(8,128)(2,1)S(1)}, bf16[1,512,1024]{2,1,0:T(8,128)(2,1)}, u32[]{:S(2)}) copy-start(bf16[1,512,1024]{2,1,0:T(8,128)(2,1)} %param.19) | copy-start | bytes 3145732
  (23 other events, 136.0 us)
Sparse Core Ops, SparseCore 0:
  10.4 64.7 all-gather.6
  77.3 40.1 all-gather.8
  119.6 72.9 all-gather.10
  194.7 72.9 all-gather.12
  315.8 70.6 reduce-scatter.9
  500.7 131.9 reduce-scatter.7
  636.7 176.6 reduce-scatter.11
  817.5 176.4 reduce-scatter.13
  998.1 55.2 reduce-scatter.15
  1056.8 50.7 all-reduce.18
where the time goes:
time: 1130 us; the launch traced here: 1120 us
  waiting for transfers between devices  512 us (45%)
  matrix products  227 us (20%)
  blocking collectives  218 us (19%)
  local copies, waits for them, and re-layouts  82.9 us (7%)
  other arithmetic  49.6 us (4%)
  between operations  17.2 us (2%)
  starting transfers between devices  14.4 us (1%)
    reduce_scatter x1, waiting for transfers between devices, per_device(): lax.psum_scatter(grad_up_weight, 'fsdp', scatter_dimension=0, tiled=True)  179 us
    reduce_scatter x1, waiting for transfers between devices, per_device(): lax.psum_scatter(grad_down_weight, 'fsdp', scatter_dimension=0, tiled=True)  178 us
    unnamed x2, blocking collectives  119 us
    dot_general x28, matrix products, right_contract(): lax.dot_general(left, right, (((1,), (1,)), ((), ())), preferred_element_...  100 us
    reduce_scatter x1, waiting for transfers between devices, per_device(): lax.psum_scatter(grad_joint_weight, 'fsdp', scatter_dimension=0, tiled=True)  79.2 us
    dot_general x20, matrix products, left_contract(): lax.dot_general(left, right, (((0,), (0,)), ((), ())), preferred_element_...  67.8 us
    dot_general x20, matrix products, matmul(): return jnp.dot(left, right, preferred_element_type=jnp.float32)  58.5 us
    all_to_all x1, blocking collectives, per_device(): lax.all_to_all(grad_stack, 'seq', split_axis=0, concat_axis=2, tiled=True)  51.4 us
  transfers between devices with their start and end apart: 13, of which 6 were waited for; matrix products, arithmetic and copies ran while one was open for 29% of the time, Pallas kernels for 0%

commit v1 on v0

v1 whole, which is shorter than its diff:
```python
import jax
import jax.numpy as jnp
from jax import lax
from jax.experimental import pallas as pl
from jax.experimental.pallas import tpu as pltpu
from jax.sharding import PartitionSpec as P

HEADS = 16
HEAD_DIM = 64
TILE = 256
EPSILON = 1e-05
FAR = 1e30


def gelu_tanh(values):
    return jax.nn.gelu(values, approximate=True)


def matmul(left, right):
    return jnp.dot(left, right, preferred_element_type=jnp.float32)


def left_contract(left, right):
    return lax.dot_general(
        left, right, (((0,), (0,)), ((), ())), preferred_element_type=jnp.float32
    )


def right_contract(left, right):
    return lax.dot_general(
        left, right, (((1,), (1,)), ((), ())), preferred_element_type=jnp.float32
    )


def standardize(values):
    center = values - jnp.mean(values, axis=-1, keepdims=True)
    spread = jnp.mean(center * center, axis=-1, keepdims=True)
    rate = lax.rsqrt(spread + EPSILON)
    return center * rate, rate


def norm_back(grad, gain, xhat, rate):
    e = grad * gain
    mean_e = jnp.mean(e, axis=-1, keepdims=True)
    mean_ex = jnp.mean(e * xhat, axis=-1, keepdims=True)
    return (e - mean_e - xhat * mean_ex) * rate


def half_starts(side, half):
    first = pl.multiple_of(side * half, half)
    second = pl.multiple_of(half - side * half, half)
    return first, second


def in_order(ref, first, second, half):
    return jnp.concatenate([ref[pl.ds(first, half), :], ref[pl.ds(second, half), :]], axis=0)


def tile_start(g, first, second, half):
    per_half = half // TILE
    base = first if g < per_half else second
    return pl.multiple_of(base + (g % per_half) * TILE, TILE)


def pad_head(x, a):
    zeros = jnp.zeros((HEAD_DIM, x.shape[1]), x.dtype)
    mine = x[a * HEAD_DIM : (a + 1) * HEAD_DIM]
    return jnp.concatenate([mine, zeros] if a == 0 else [zeros, mine], axis=0)


def attend_kernel(side_ref, slope_ref, q_ref, k_ref, v_ref, far_ref, out_ref, log_ref):
    length = q_ref.shape[0]
    half = length // 2
    pair = pl.program_id(0)
    first, second = half_starts(side_ref[0], half)
    keys = in_order(k_ref, first, second, half)
    values_t = in_order(v_ref, first, second, half).T
    for g in range(length // TILE):
        reach = min((g + 2) * TILE, length)
        start = tile_start(g, first, second, half)
        queries_t = (q_ref[pl.ds(start, TILE), :] * jnp.bfloat16(HEAD_DIM ** (-0.5))).T
        pieces = []
        for a in range(2):
            slope = slope_ref[2 * pair + a]
            scores = matmul(keys[:reach], pad_head(queries_t, a))
            scores = scores - slope * far_ref[:reach, g * TILE : (g + 1) * TILE]
            top = jnp.max(scores, axis=0, keepdims=True)
            weights = jnp.exp(scores - top)
            total = jnp.sum(weights, axis=0, keepdims=True)
            mixed_t = matmul(
                values_t[a * HEAD_DIM : (a + 1) * HEAD_DIM, :reach], weights.astype(jnp.bfloat16)
            )
            pieces.append(mixed_t / total)
            log_ref[0, a : a + 1, g * TILE : (g + 1) * TILE] = top + jnp.log(total)
        out_ref[pl.ds(start, TILE), :] = jnp.concatenate(pieces, axis=0).T.astype(jnp.bfloat16)


def attend_heads(joint, side, slopes, far):
    length, width = joint.shape
    pairs = width // 3 // 128
    whole = lambda offset: pl.BlockSpec((length, 128), lambda p, s: (0, p + offset))
    return pl.pallas_call(
        attend_kernel,
        grid_spec=pltpu.PrefetchScalarGridSpec(
            num_scalar_prefetch=1,
            grid=(pairs,),
            in_specs=[
                pl.BlockSpec(memory_space=pltpu.SMEM),
                whole(0),
                whole(pairs),
                whole(2 * pairs),
                pl.BlockSpec((length, length), lambda p, s: (0, 0)),
            ],
            out_specs=[
                pl.BlockSpec((length, 128), lambda p, s: (0, p)),
                pl.BlockSpec((1, 2, length), lambda p, s: (p, 0, 0)),
            ],
        ),
        out_shape=[
            jax.ShapeDtypeStruct((length, width // 3), jnp.bfloat16),
            jax.ShapeDtypeStruct((pairs, 2, length), jnp.float32),
        ],
        compiler_params=pltpu.CompilerParams(vmem_limit_bytes=48 << 20),
        name="attend",
    )(side, slopes, joint, joint, joint, far)


def back_kernel(
    side_ref,
    slope_ref,
    q_ref,
    k_ref,
    v_ref,
    far_ref,
    log_ref,
    mixed_ref,
    grad_ref,
    out_ref,
    dq_ref,
    dk_ref,
    dv_ref,
):
    length = q_ref.shape[0]
    half = length // 2
    pair = pl.program_id(0)
    part = pl.program_id(1)
    first, second = half_starts(side_ref[0], half)
    factor = HEAD_DIM ** (-0.5)

    @pl.when(part == 0)
    def _():
        keys = in_order(k_ref, first, second, half)
        keys_t = keys.T
        values = in_order(v_ref, first, second, half)
        lane = lax.broadcasted_iota(jnp.int32, (TILE, 128), 1)
        dk_ref[...] = jnp.zeros_like(dk_ref)
        dv_ref[...] = jnp.zeros_like(dv_ref)
        for g in range(length // TILE):
            reach = min((g + 2) * TILE, length)
            start = tile_start(g, first, second, half)
            queries = q_ref[pl.ds(start, TILE), :] * jnp.bfloat16(factor)
            queries_t = queries.T
            grads = grad_ref[pl.ds(start, TILE), :]
            grads_t = grads.T
            product = grads.astype(jnp.float32) * mixed_ref[pl.ds(start, TILE), :].astype(
                jnp.float32
            )
            product_t = product.T
            pieces = []
            for a in range(2):
                rows = slice(a * HEAD_DIM, (a + 1) * HEAD_DIM)
                slope = slope_ref[2 * pair + a]
                own = (lane < HEAD_DIM) if a == 0 else (lane >= HEAD_DIM)
                scores = matmul(keys[:reach], pad_head(queries_t, a))
                scores = scores - slope * far_ref[:reach, g * TILE : (g + 1) * TILE]
                probs = jnp.exp(scores - log_ref[0, a : a + 1, g * TILE : (g + 1) * TILE])
                grad_probs = matmul(values[:reach], pad_head(grads_t, a))
                inner = jnp.sum(product_t[rows], axis=0, keepdims=True)
                grad_scores = (probs * (grad_probs - inner)).astype(jnp.bfloat16)
                zero = jnp.zeros((), jnp.bfloat16)
                dk_ref[:reach] += matmul(grad_scores, jnp.where(own, queries, zero))
                dv_ref[:reach] += matmul(probs.astype(jnp.bfloat16), jnp.where(own, grads, zero))
                pieces.append(matmul(keys_t[rows, :reach], grad_scores))
            both = jnp.concatenate(pieces, axis=0).T * factor
            dq_ref[pl.ds(start, TILE), :] = both.astype(jnp.bfloat16)
        out_ref[...] = dq_ref[...]

    @pl.when(part == 1)
    def _():
        out_ref[pl.ds(first, half), :] = dk_ref[:half].astype(jnp.bfloat16)
        out_ref[pl.ds(second, half), :] = dk_ref[half:].astype(jnp.bfloat16)

    @pl.when(part == 2)
    def _():
        out_ref[pl.ds(first, half), :] = dv_ref[:half].astype(jnp.bfloat16)
        out_ref[pl.ds(second, half), :] = dv_ref[half:].astype(jnp.bfloat16)


def attend_back(joint, side, slopes, far, logs, mixed, grads):
    length, width = joint.shape
    pairs = width // 3 // 128
    whole = lambda offset: pl.BlockSpec((length, 128), lambda p, t, s: (0, p + offset))
    return pl.pallas_call(
        back_kernel,
        grid_spec=pltpu.PrefetchScalarGridSpec(
            num_scalar_prefetch=1,
            grid=(pairs, 3),
            in_specs=[
                pl.BlockSpec(memory_space=pltpu.SMEM),
                whole(0),
                whole(pairs),
                whole(2 * pairs),
                pl.BlockSpec((length, length), lambda p, t, s: (0, 0)),
                pl.BlockSpec((1, 2, length), lambda p, t, s: (p, 0, 0)),
                whole(0),
                whole(0),
            ],
            out_specs=pl.BlockSpec((length, 128), lambda p, t, s: (0, t * pairs + p)),
            scratch_shapes=[
                pltpu.VMEM((length, 128), jnp.bfloat16),
                pltpu.VMEM((length, 128), jnp.float32),
                pltpu.VMEM((length, 128), jnp.float32),
            ],
        ),
        out_shape=jax.ShapeDtypeStruct((length, width), jnp.bfloat16),
        compiler_params=pltpu.CompilerParams(vmem_limit_bytes=48 << 20),
        name="attend_back",
    )(side, slopes, joint, joint, joint, far, logs, mixed, grads)


def per_device(
    tokens,
    blocks,
    first_gain,
    first_shift,
    joint_weight,
    joint_bias,
    output_weight,
    output_bias,
    second_gain,
    second_shift,
    upward_weight,
    upward_bias,
    downward_weight,
    downward_bias,
    cotangent,
):
    groups = lax.axis_size("seq")
    shards = lax.axis_size("fsdp")
    side = lax.axis_index("seq")
    half_tokens = tokens.shape[1]
    width = tokens.shape[2]
    rows = joint_weight.shape[0]
    length = half_tokens * groups
    local_heads = HEADS // groups
    part = width // groups
    hidden_rows = downward_weight.shape[0]
    unit = hidden_rows // groups
    wide = 3 * part
    f32 = jnp.float32
    bf16 = jnp.bfloat16

    def swap(x):
        return lax.ppermute(x, "seq", [(s, groups - 1 - s) for s in range(groups)])

    def pick(x, axis, which=side):
        return lax.dynamic_index_in_dim(x, which, axis, keepdims=False)

    def gather(x):
        return lax.all_gather(x, "fsdp", axis=0, tiled=True)

    def scatter(x):
        return lax.psum_scatter(x, "fsdp", scatter_dimension=0, tiled=True)

    def weave(own, other, axis):
        return jnp.where(
            side == 0, jnp.stack([own, other], axis), jnp.stack([other, own], axis)
        )

    token_own = tokens[0]
    grad_own = cotangent[0]
    token_other = swap(token_own)
    grad_other = swap(grad_own)

    vectors = jnp.concatenate(
        [
            first_gain,
            first_shift,
            joint_bias[0],
            joint_bias[1],
            output_bias,
            second_gain,
            second_shift,
            downward_bias,
            upward_bias,
        ]
    )
    vector_rows = 16
    vector_block = jnp.pad(
        vectors[None], ((0, vector_rows - 1), (0, wide - vectors.shape[0]))
    )
    joint_part = pick(joint_weight.reshape(rows, 3, groups, part), 2).reshape(rows, wide)
    packed = gather(jnp.concatenate([joint_part, vector_block], axis=0))
    packed = packed.reshape(shards, rows + vector_rows, wide)
    joint_full = packed[:, :rows].reshape(width, wide)
    vector_full = packed[:, rows].astype(f32)
    out_full = gather(output_weight)
    up_part = pick(upward_weight.reshape(rows, shards, groups, unit), 2)
    up_full = gather(up_part.reshape(rows, shards * unit))
    down_full = gather(pick(downward_weight.reshape(groups, unit, width), 0))

    def vector(index):
        return vector_full[:, index * rows : (index + 1) * rows].reshape(width)

    gain_one, shift_one, query_bias, value_bias = (vector(n) for n in range(4))
    out_bias, gain_two, shift_two, down_bias = (vector(n) for n in range(4, 8))
    up_bias = vector_full[:, 8 * rows : 8 * rows + hidden_rows].reshape(shards, groups, unit)
    up_bias = pick(up_bias, 1).reshape(shards * unit)
    joint_bias_part = jnp.concatenate(
        [
            pick(query_bias.reshape(groups, part), 0),
            jnp.zeros((part,), f32),
            pick(value_bias.reshape(groups, part), 0),
        ]
    )

    inputs = jnp.concatenate([token_own, token_other], axis=0).astype(f32)
    xhat_one, rate_one = standardize(inputs)
    normed_one = (xhat_one * gain_one + shift_one).astype(bf16)
    joint = (matmul(normed_one, joint_full) + joint_bias_part).astype(bf16)

    positions = jnp.arange(length)
    distance = jnp.abs(positions[:, None] - positions[None, :]).astype(f32)
    block_row = blocks[0]
    far = jnp.where(block_row[:, None] <= block_row[None, :], distance, FAR)
    head_index = side * local_heads + jnp.arange(local_heads)
    slopes = jnp.exp2(-8.0 * (head_index.astype(f32) + 1.0) / HEADS)
    side_array = side.astype(jnp.int32).reshape(1)
    mixed_own, logs = attend_heads(joint, side_array, slopes, far)

    mixed_other = swap(mixed_own)
    mixed_other = jnp.concatenate([mixed_other[half_tokens:], mixed_other[:half_tokens]], axis=0)
    mixed = jnp.concatenate([mixed_own, mixed_other], axis=1)
    out_parts = out_full.reshape(groups, part, width)
    out_turned = jnp.concatenate([pick(out_parts, 0), pick(out_parts, 0, groups - 1 - side)], axis=0)
    hidden = inputs + matmul(mixed, out_turned) + out_bias
    xhat_two, rate_two = standardize(hidden)
    normed_two = (xhat_two * gain_two + shift_two).astype(bf16)
    upward = matmul(normed_two, up_full) + up_bias
    activated = gelu_tanh(upward).astype(bf16)

    grad_low = jnp.concatenate([grad_own, grad_other], axis=0)
    grad_down = left_contract(activated, grad_low).astype(bf16)
    grad_down = scatter(grad_down)
    grad_act = right_contract(grad_low, down_full)
    grad_up = jax.vjp(gelu_tanh, upward)[1](grad_act)[0].astype(bf16)
    grad_up_weight = scatter(left_contract(normed_two, grad_up).astype(bf16))
    grad_two = right_contract(grad_up, up_full)
    grad_two_own = grad_two[:half_tokens] + swap(grad_two[half_tokens:].astype(bf16)).astype(f32)
    grad_hidden = grad_own.astype(f32) + norm_back(
        grad_two_own, gain_two, xhat_two[:half_tokens], rate_two[:half_tokens]
    )
    hidden_low = grad_hidden.astype(bf16)

    grad_mixed = right_contract(hidden_low, out_turned).astype(bf16)
    grad_heads = jnp.concatenate([grad_mixed[:, :part], swap(grad_mixed[:, part:])], axis=0)
    grad_joint = attend_back(joint, side_array, slopes, far, logs, mixed_own, grad_heads)

    low_parts = hidden_low.reshape(half_tokens, groups, part)
    low_columns = jnp.concatenate(
        [pick(low_parts, 1), swap(pick(low_parts, 1, groups - 1 - side))], axis=0
    )
    grad_out = left_contract(mixed, low_columns).astype(bf16)
    out_rows = grad_out.reshape(groups, part, part)
    grad_out = jnp.concatenate([pick(out_rows, 0), pick(out_rows, 0, groups - 1 - side)], axis=0)
    grad_out = scatter(grad_out)

    partial_out = matmul(activated, down_full)
    result_other = swap(partial_out[half_tokens:].astype(bf16)).astype(f32)
    result = hidden[:half_tokens] + partial_out[:half_tokens] + result_other + down_bias

    grad_joint_weight = left_contract(normed_one, grad_joint).astype(bf16)
    grad_one = right_contract(grad_joint, joint_full)

    def spread(x):
        empty = jnp.zeros_like(x)
        return weave(x, empty, 0).reshape(width)

    joint_sums = jnp.sum(grad_joint.astype(f32), axis=0)
    sums = [
        jnp.sum(grad_one * xhat_one, axis=0),
        jnp.sum(grad_one, axis=0),
        spread(joint_sums[:part]),
        spread(joint_sums[2 * part :]),
        jnp.sum(hidden_low.astype(f32), axis=0),
        jnp.sum(grad_two * xhat_two, axis=0),
        jnp.sum(grad_two, axis=0),
        jnp.sum(grad_own.astype(f32), axis=0),
    ]
    up_sums = jnp.sum(grad_up.astype(f32), axis=0).reshape(shards, unit)
    up_sums = weave(up_sums, jnp.zeros_like(up_sums), 1).reshape(shards, hidden_rows)
    sum_rows = jnp.concatenate([s.reshape(shards, rows) for s in sums] + [up_sums], axis=1)
    sum_rows = sum_rows.astype(bf16)
    sum_block = jnp.pad(
        sum_rows[:, None],
        ((0, 0), (0, vector_rows - 1), (0, wide - sum_rows.shape[1])),
    )
    last = jnp.concatenate([grad_joint_weight.reshape(shards, rows, wide), sum_block], axis=1)
    last = scatter(last.reshape(shards * (rows + vector_rows), wide))

    grad_one_own = grad_one[:half_tokens] + swap(grad_one[half_tokens:].astype(bf16)).astype(f32)
    grad_tokens = grad_hidden + norm_back(
        grad_one_own, gain_one, xhat_one[:half_tokens], rate_one[:half_tokens]
    )

    down_total = weave(grad_down, swap(grad_down), 0).reshape(hidden_rows, width)
    up_own = grad_up_weight.reshape(rows, shards, unit)
    up_other = swap(grad_up_weight).reshape(rows, shards, unit)
    up_total = weave(up_own, up_other, 2).reshape(rows, shards * hidden_rows)
    out_total = weave(grad_out, swap(grad_out), 1).reshape(rows, width)
    last_other = swap(last)
    joint_total = weave(
        last[:rows].reshape(rows, 3, part), last_other[:rows].reshape(rows, 3, part), 2
    ).reshape(rows, 3 * width)
    vector_total = last[rows].astype(f32) + last_other[rows].astype(f32)

    def total(index):
        return vector_total[index * rows : (index + 1) * rows]

    return (
        result.astype(bf16)[None],
        grad_tokens[None],
        total(0),
        total(1),
        joint_total.astype(f32),
        jnp.stack([total(2), total(3)]),
        out_total.astype(f32),
        total(4),
        total(5),
        total(6),
        up_total.astype(f32),
        vector_total[8 * rows : 8 * rows + hidden_rows],
        down_total.astype(f32),
        total(7),
    )


def solution(mesh):
    in_specs = (
        P("fsdp", "seq", None),
        P("fsdp", None),
        P("fsdp"),
        P("fsdp"),
        P("fsdp", None),
        P(None, "fsdp"),
        P("fsdp", None),
        P("fsdp"),
        P("fsdp"),
        P("fsdp"),
        P("fsdp", None),
        P("fsdp"),
        P("fsdp", None),
        P("fsdp"),
        P("fsdp", "seq", None),
    )
    out_specs = (
        P("fsdp", "seq", None),
        P("fsdp", "seq", None),
        P("fsdp"),
        P("fsdp"),
        P("fsdp", None),
        P(None, "fsdp"),
        P("fsdp", None),
        P("fsdp"),
        P("fsdp"),
        P("fsdp"),
        P("fsdp", None),
        P("fsdp"),
        P("fsdp", None),
        P("fsdp"),
    )
    return jax.shard_map(
        per_device, mesh=mesh, in_specs=in_specs, out_specs=out_specs, check_vma=False
    )
```

time: 1130 us -> 580 us (0.51)
  blocking collectives: 218 us -> 0 us
  waiting for transfers between devices: 512 us -> 320 us
  matrix products: 227 us -> 87.9 us
  Pallas kernels: 0 us -> 49.3 us
  local copies, waits for them, and re-layouts: 82.9 us -> 49.4 us
  other arithmetic: 49.6 us -> 35.1 us
    reduce_scatter x4, waiting for transfers between devices: 437 us -> 117 us  [scatter(): return lax.psum_scatter(x, 'fsdp', scatter_dimension=0, tiled=True)]
    unnamed x2 -> x0, blocking collectives: 119 us -> none
    ppermute x0 -> x12, waiting for transfers between devices: none -> 118 us  [swap(): return lax.ppermute(x, 'seq', [(s, groups - 1 - s) for s in range(groups)])]
    all_gather x4, waiting for transfers between devices: 0.05 us -> 83.2 us  [gather(): return lax.all_gather(x, 'fsdp', axis=0, tiled=True)]
    dot_general x28 -> x4, matrix products: 100 us -> 26.3 us  [right_contract(): lax.dot_general(left, right, (((1,), (1,)), ((), ())), preferred_element_...]
    all_to_all x1 -> x0, blocking collectives: 51.4 us -> none  [per_device(): lax.all_to_all(grad_stack, 'seq', split_axis=0, concat_axis=2, tiled=True)]
    pallas_call x0 -> x2, Pallas kernels: none -> 49.3 us  [the longest x1 25.3 us: attend_back(): pl.pallas_call(back_kernel, grid_spec=pltpu.PrefetchScalarGridSpec(num_sc...]
    all_to_all x3 -> x0, waiting for transfers between devices: 42.6 us -> none  [the longest x1 31.7 us: per_device(): lax.all_to_all(joint, 'seq', split_axis=2, concat_axis=0, tiled=True)]
  transfers between devices with their start and end apart: 13 -> 20, of which waited for: 6 -> 14; matrix products, arithmetic and copies ran while one was open for 29% -> 23% of each run, Pallas kernels for 0% -> 9%
where the time goes in v1:
time: 580 us; the launch traced here: 576 us
  waiting for transfers between devices  320 us (55%)
  matrix products  87.9 us (15%)
  local copies, waits for them, and re-layouts  49.4 us (9%)
  Pallas kernels  49.3 us (8%)
  other arithmetic  35.1 us (6%)
  starting transfers between devices  18.9 us (3%)
  between operations  15.1 us (3%)
    ppermute x12, waiting for transfers between devices, swap(): return lax.ppermute(x, 'seq', [(s, groups - 1 - s) for s in range(groups)])  118 us
    reduce_scatter x4, waiting for transfers between devices, scatter(): return lax.psum_scatter(x, 'fsdp', scatter_dimension=0, tiled=True)  117 us
    all_gather x4, waiting for transfers between devices, gather(): return lax.all_gather(x, 'fsdp', axis=0, tiled=True)  83.2 us
    dot_general x4, matrix products, matmul(): return jnp.dot(left, right, preferred_element_type=jnp.float32)  31.6 us
    dot_general x4, matrix products, left_contract(): lax.dot_general(left, right, (((0,), (0,)), ((), ())), preferred_element_...  30.1 us
    dot_general x4, matrix products, right_contract(): lax.dot_general(left, right, (((1,), (1,)), ((), ())), preferred_element_...  26.3 us
    pallas_call x1, Pallas kernels, attend_back(): pl.pallas_call(back_kernel, grid_spec=pltpu.PrefetchScalarGridSpec(num_sc...  25.3 us
    pallas_call x1, Pallas kernels, attend_heads(): pl.pallas_call(attend_kernel, grid_spec=pltpu.PrefetchScalarGridSpec(num_...  24 us
  transfers between devices with their start and end apart: 20, of which 14 were waited for; matrix products, arithmetic and copies ran while one was open for 23% of the time, Pallas kernels for 9%

profile of v1, /device:TPU:0, one launch (start us, length us, event | category | flops | bytes accessed | tf_op | source)
XLA Modules:
  0.0 575.7 jit_solution(17119177918657556432)
XLA Ops:
  28.2 19.4 %collective-permute-done = bf16[512,1024]{0,1:T(8,128)(2,1)S(1)} collective-permute-done((bf16[512,1024]{0,1:T(8,128)(2,1)S(1)}, bf16[512,1024]{0,1:T(8,128)(2,1)S(1)}, u32[]{:S(2)}, u32[]{:S(2)}) %collective-permute-start) | collective-permute-done | bytes 1048608 | tf_op jit(solution)/shard_map/ppermute | solution.py:264
  48.5 19.6 %all-gather.6.cloned.1.call-done = bf16[1280,1536]{1,0:T(8,128)(2,1)} async-done(((bf16[80,1536]{1,0:T(8,128)(2,1)}), bf16[1280,1536]{1,0:T(8,128)(2,1)}) %all-gather.6.cloned.1.call-update) | async-done | bytes 3932176 | tf_op jit(solution)/shard_map/all_gather | solution.py:270
  73.4 6.3 %add_convert_fusion.q_ref.k_ref.v_ref = bf16[1024,1536]{1,0:T(8,128)(2,1)S(1)} fusion(bf16[1024,1536]{1,0:T(8,128)(2,1)} %bitcast.116, f32[1536]{0:T(1024)S(1)} %pad_maximum_fusion.9, f32[1024]{0:T(1024)S(1)} %add.181, f32[1024]{0:T(1024)S(1)} %mul.157, f32[1024]{0:T(1024)S(1)} %add_rsqrt_fusion.1, f32[1024]{0:T(1024)S(1)} %broadcast_multiply_fusion.1, ...), kind=kOutput, calls=%fused_computation.14 | convolution fusion | flops 3233808384 | bytes 8411136 | tf_op jit(solution)/shard_map/dot_general | solution.py:20
  79.7 24.0 %attend.1 = (bf16[1024,512]{1,0:T(8,128)(2,1)}, f32[4,2,1024]{2,1,0:T(2,128)S(1)}) custom-call(s32[1]{0:T(128)} %bitcast.1.side_ref, f32[8]{0:T(128)S(1)} %multiply_exponential_fusion.slope_ref, bf16[1024,1536]{1,0:T(8,128)(2,1)S(1)} %add_convert_fusion.q_ref.k_ref.v_ref, bf16[1024,1536]{1,0:T(8,128)(2,1)S(1)} %add_convert_fusion.q_ref.k_ref.v_ref, ...), custom_call_target="tpu_custom_call" | custom-call | tf_op jit(solution)/shard_map/attend/pallas_call | solution.py:102
  113.6 16.4 %collective-permute-done.1 = bf16[1024,512]{1,0:T(8,128)(2,1)} collective-permute-done((bf16[1024,512]{1,0:T(8,128)(2,1)}, bf16[1024,512]{1,0:T(8,128)(2,1)}, u32[]{:S(2)}, u32[]{:S(2)}) %collective-permute-start.1) | collective-permute-done | bytes 1048608 | tf_op jit(solution)/shard_map/ppermute | solution.py:264
  140.8 20.9 %all-gather.10.cloned.1.call-done = bf16[1024,2048]{1,0:T(8,128)(2,1)} async-done(((bf16[64,2048]{1,0:T(8,128)(2,1)}), bf16[1024,2048]{1,0:T(8,128)(2,1)}) %all-gather.10.cloned.1.call-update) | async-done | bytes 4194320 | tf_op jit(solution)/shard_map/all_gather | solution.py:270
  161.7 11.5 %fusion.40 = f32[1024,2048]{1,0:T(8,128)} fusion(bf16[1024,2048]{1,0:T(8,128)(2,1)} %all-gather.10.cloned.1.call-done, f32[1024,1024]{0,1:T(8,128)} %subtract_multiply_fusion, f32[1024]{0:T(1024)S(1)} %add.192, f32[1024]{0:T(1024)S(1)} %mul.163), kind=kOutput, calls=%fused_computation.122 | convolution fusion | flops 4298113024 | bytes 16785408 | tf_op jit(solution)/shard_map/dot_general | solution.py:20
  173.2 40.0 %all-gather.12.cloned.1.call-done = bf16[1,2048,1024]{2,1,0:T(8,128)(2,1)} async-done(((bf16[1,128,1024]{2,1,0:T(8,128)(2,1)}), bf16[1,2048,1024]{2,1,0:T(8,128)(2,1)}) %all-gather.12.cloned.1.call-update) | async-done | bytes 4194320 | tf_op jit(solution)/shard_map/all_gather | solution.py:270
  213.2 14.0 %convert_reduce_fusion = (f32[2048]{0:T(1024)S(1)}, bf16[1024,2048]{1,0:T(8,128)(2,1)S(1)}) fusion(f32[1024,2048]{1,0:T(8,128)} %fusion.40, f32[2048]{0:T(1024)S(1)} %bitcast.139, bf16[1,2048,1024]{2,1,0:T(8,128)(2,1)} %all-gather.12.cloned.1.call-done, bf16[512,1024]{0,1:T(8,128)(2,1)} %collective-permute-done.3, bf16[512,1024]{0,1:T(8,128)(2,1)S(1)} %bitcast.112), kind=kOutput, calls=%fused_computation.9 | convolution fusion | flops 4347394048 | bytes 18890752 | tf_op jit(solution)/shard_map/dot_general | solution.py:30
  233.6 23.8 %collective-permute-done.4 = bf16[512,1024]{0,1:T(8,128)(2,1)S(1)} collective-permute-done((bf16[512,1024]{0,1:T(8,128)(2,1)S(1)}, bf16[512,1024]{0,1:T(8,128)(2,1)S(1)}, u32[]{:S(2)}, u32[]{:S(2)}) %collective-permute-start.4) | collective-permute-done | bytes 1048608 | tf_op jit(solution)/shard_map/ppermute | solution.py:264
  260.6 11.7 %collective-permute-done.8 = bf16[512,512]{0,1:T(8,128)(2,1)S(1)} collective-permute-done((bf16[512,512]{0,1:T(8,128)(2,1)S(1)}, bf16[512,512]{0,1:T(8,128)(2,1)S(1)}, u32[]{:S(2)}, u32[]{:S(2)}) %collective-permute-start.8) | collective-permute-done | bytes 524320 | tf_op jit(solution)/shard_map/ppermute | solution.py:264
  276.3 10.0 %convolution_convert_fusion.2 = bf16[1024,2048]{1,0:T(8,128)(2,1)} fusion(bf16[1024,2048]{1,0:T(8,128)(2,1)} %copy-done.29, f32[1024,1024]{0,1:T(8,128)} %subtract_multiply_fusion, f32[1024]{0:T(1024)S(1)} %add.192, f32[1024]{0:T(1024)S(1)} %mul.163), kind=kOutput, calls=%fused_computation.36 | convolution fusion | flops 4300210176 | bytes 12591104 | tf_op jit(solution)/shard_map/dot_general | solution.py:24
  286.4 12.5 %convolution_convert_fusion.1 = bf16[2048,1024]{1,0:T(8,128)(2,1)} fusion(bf16[512,1024]{0,1:T(8,128)(2,1)} %collective-permute-done.3, bf16[512,1024]{0,1:T(8,128)(2,1)S(1)} %bitcast.113, f32[1024,2048]{1,0:T(8,128)} %fusion.40, f32[2048]{0:T(1024)S(1)} %bitcast.140), kind=kOutput, calls=%fused_computation.35 | convolution fusion | flops 4322230272 | bytes 14688256 | tf_op jit(solution)/shard_map/dot_general | solution.py:24
  304.9 10.4 %collective-permute-done.5 = bf16[512,512]{1,0:T(8,128)(2,1)S(1)} collective-permute-done((bf16[512,512]{1,0:T(8,128)(2,1)S(1)}, bf16[512,512]{1,0:T(8,128)(2,1)S(1)}, u32[]{:S(2)}, u32[]{:S(2)}) %collective-permute-start.5) | collective-permute-done | bytes 524320 | tf_op jit(solution)/shard_map/ppermute | solution.py:264
  315.3 25.3 %attend_back.1 = bf16[1024,1536]{1,0:T(8,128)(2,1)S(1)} custom-call(s32[1]{0:T(128)} %bitcast.1.side_ref, f32[8]{0:T(128)S(1)} %multiply_exponential_fusion.slope_ref, bf16[1024,1536]{1,0:T(8,128)(2,1)} %copy-done.2, bf16[1024,1536]{1,0:T(8,128)(2,1)} %copy-done.2, bf16[1024,1536]{1,0:T(8,128)(2,1)} %copy-done.2, f32[1024,1024]{1,0:T(8,128)} %convert_select_fusion.far_ref, ...), custom_call_target="tpu_custom_call" | custom-call | tf_op jit(solution)/shard_map/attend_back/pallas_call | solution.py:203
  340.6 5.1 fusion.50
  345.7 5.6 copy.89
  351.3 5.8 %multiply_reduce_fusion.1 = (bf16[1024]{0:T(1024)(128)(2,1)S(1)}, f32[1024,1024]{0,1:T(8,128)}) fusion(f32[1024,1024]{0,1:T(8,128)} %copy.89, f32[1024]{0:T(1024)S(1)} %add_rsqrt_fusion.1, f32[1024]{0:T(1024)S(1)} %broadcast_multiply_fusion.1, bf16[512,1024]{0,1:T(8,128)(2,1)} %copy-done.8, bf16[512,1024]{0,1:T(8,128)(2,1)} %bitcast.107), kind=kLoop, calls=%fused_computation.27 | loop fusion | flops 8387584 | bytes 10496000 | tf_op jit(solution)/shard_map/reduce_sum | solution.py:391
  365.2 8.9 %fusion.14 = f32[1024,1024]{0,1:T(8,128)S(1)} fusion(bf16[1,2048,1024]{2,1,0:T(8,128)(2,1)} %all-gather.12.cloned.1.call-done, f32[1024,2048]{1,0:T(8,128)} %fusion.40, f32[2048]{0:T(1024)S(1)} %bitcast.141), kind=kOutput, calls=%fused_computation.24 | convolution fusion | flops 4315938816 | bytes 16785408 | tf_op jit(solution)/shard_map/dot_general | solution.py:20
  380.3 20.0 %collective-permute-done.2 = bf16[512,1024]{0,1:T(8,128)(2,1)S(1)} collective-permute-done((bf16[512,1024]{0,1:T(8,128)(2,1)S(1)}, bf16[512,1024]{0,1:T(8,128)(2,1)S(1)}, u32[]{:S(2)}, u32[]{:S(2)}) %collective-permute-start.2) | collective-permute-done | bytes 1048608 | tf_op jit(solution)/shard_map/ppermute | solution.py:264
  406.3 13.9 %collective-permute-done.6 = bf16[512,1024]{0,1:T(8,128)(2,1)S(1)} collective-permute-done((bf16[512,1024]{0,1:T(8,128)(2,1)}, bf16[512,1024]{0,1:T(8,128)(2,1)S(1)}, u32[]{:S(2)}, u32[]{:S(2)}) %collective-permute-start.6) | collective-permute-done | bytes 1048608 | tf_op jit(solution)/shard_map/ppermute | solution.py:264
  425.2 58.4 %reduce-scatter.11.cloned.1.call-done = bf16[128,1024]{1,0:T(8,128)(2,1)} async-done(((bf16[2048,1024]{1,0:T(8,128)(2,1)}), bf16[128,1024]{1,0:T(8,128)(2,1)}) %reduce-scatter.11.cloned.1.call-update) | async-done | bytes 262160 | tf_op jit(solution)/shard_map/reduce_scatter | solution.py:273
  485.2 5.1 add_bitcast_fusion
  498.1 59.0 %reduce-scatter.5.cloned.1.call-done = bf16[80,1536]{1,0:T(8,128)(2,1)} async-done(((bf16[1280,1536]{1,0:T(8,128)(2,1)}), bf16[80,1536]{1,0:T(8,128)(2,1)}) %reduce-scatter.5.cloned.1.call-update) | async-done | bytes 245776 | tf_op jit(solution)/shard_map/reduce_scatter | solution.py:273
  (205 shorter events, 113.1 us)
Async XLA Ops:
  7.2 60.9 %all-gather.6.cloned.1.call-start = ((), (), s32[]{:S(2)}) async-start(), calls=%async_computation.4 | async-start | bytes 4177920 | tf_op jit(solution)/shard_map/all_gather | solution.py:270
  16.2 94.2 %all-gather.8.cloned.1.call-start = ((), (), s32[]{:S(2)}) async-start(), calls=%async_computation.5 | async-start | bytes 2228224 | tf_op jit(solution)/shard_map/all_gather | solution.py:270
  16.9 144.7 %all-gather.10.cloned.1.call-start = ((), (), s32[]{:S(2)}) async-start(), calls=%async_computation.6 | async-start | bytes 4456448 | tf_op jit(solution)/shard_map/all_gather | solution.py:270
  20.7 192.5 %all-gather.12.cloned.1.call-start = ((), (), s32[]{:S(2)}) async-start(), calls=%async_computation.11 | async-start | bytes 4456448 | tf_op jit(solution)/shard_map/all_gather | solution.py:270
  21.3 26.2 %collective-permute-start = (bf16[512,1024]{0,1:T(8,128)(2,1)S(1)}, bf16[512,1024]{0,1:T(8,128)(2,1)S(1)}, u32[]{:S(2)}, u32[]{:S(2)}) collective-permute-start(bf16[512,1024]{0,1:T(8,128)(2,1)S(1)} %bitcast.103), channel_id=1, source_target_pairs={{0,16},{16,0},{1,17},{17,1},{2,18},{18,2},{3,19},{19,3},{4,20},{20... | collective-permute-start | bytes 3145736 | tf_op jit(solution)/shard_map/ppermute | solution.py:264
  25.1 398.0 %reduce-scatter.7.cloned.1.call-start = ((), (), s32[]{:S(2)}) async-start(), calls=%async_computation.8 | async-start | bytes 1114112 | tf_op jit(solution)/shard_map/reduce_scatter | solution.py:273
  48.5 331.7 %copy-start.26 = (f32[1024]{0:T(1024)}, f32[1024]{0:T(1024)S(1)}, u32[]{:S(2)}) copy-start(f32[1024]{0:T(1024)S(1)} %add_rsqrt_fusion.1) | copy-start | bytes 12292
  103.6 26.4 %collective-permute-start.1 = (bf16[1024,512]{1,0:T(8,128)(2,1)}, bf16[1024,512]{1,0:T(8,128)(2,1)}, u32[]{:S(2)}, u32[]{:S(2)}) collective-permute-start(bf16[1024,512]{1,0:T(8,128)(2,1)} %get-tuple-element.16.mixed_ref), channel_id=1, source_target_pairs={{0,16},{16,0},{1,17},{17,1},{2,18},{18,2},{3,19},{19,3},{4,20},{20... | collective-permute-start | bytes 3145736 | tf_op jit(solution)/shard_map/ppermute | solution.py:264
  106.9 179.5 %copy-start.12 = (bf16[1,512,1024]{1,2,0:T(8,128)(2,1)}, bf16[1,512,1024]{1,2,0:T(8,128)(2,1)S(1)}, u32[]{:S(2)}) copy-start(bf16[1,512,1024]{1,2,0:T(8,128)(2,1)S(1)} %copy.88) | copy-start | bytes 3145732
  106.9 66.3 %collective-permute-start.3 = (bf16[512,1024]{0,1:T(8,128)(2,1)S(1)}, bf16[512,1024]{0,1:T(8,128)(2,1)}, u32[]{:S(2)}, u32[]{:S(2)}) collective-permute-start(bf16[512,1024]{0,1:T(8,128)(2,1)S(1)} %bitcast.111), channel_id=1, source_target_pairs={{0,16},{16,0},{1,17},{17,1},{2,18},{18,2},{3,19},{19,3},{4,20},{20... | collective-permute-start | bytes 3145736 | tf_op jit(solution)/shard_map/ppermute | solution.py:264
  232.1 25.4 %collective-permute-start.4 = (bf16[512,1024]{0,1:T(8,128)(2,1)S(1)}, bf16[512,1024]{0,1:T(8,128)(2,1)S(1)}, u32[]{:S(2)}, u32[]{:S(2)}) collective-permute-start(bf16[512,1024]{0,1:T(8,128)(2,1)S(1)} %slice.305), channel_id=1, source_target_pairs={{0,16},{16,0},{1,17},{17,1},{2,18},{18,2},{3,19},{19,3},{4,20},{20... | collective-permute-start | bytes 3145736 | tf_op jit(solution)/shard_map/ppermute | solution.py:264
  259.1 13.3 %collective-permute-start.8 = (bf16[512,512]{0,1:T(8,128)(2,1)S(1)}, bf16[512,512]{0,1:T(8,128)(2,1)S(1)}, u32[]{:S(2)}, u32[]{:S(2)}) collective-permute-start(bf16[512,512]{0,1:T(8,128)(2,1)S(1)} %get-tuple-element.103), channel_id=1, source_target_pairs={{0,16},{16,0},{1,17},{17,1},{2,18},{18,2},{3,19},{19,3},{4,20},{20... | collective-permute-start | bytes 1572872 | tf_op jit(solution)/shard_map/ppermute | solution.py:264
  276.1 148.6 %reduce-scatter.9.cloned.1.call-start = ((), (), s32[]{:S(2)}) async-start(), calls=%async_computation.9 | async-start | bytes 4456448 | tf_op jit(solution)/shard_map/reduce_scatter | solution.py:273
  286.3 197.3 %reduce-scatter.11.cloned.1.call-start = ((), (), s32[]{:S(2)}) async-start(), calls=%async_computation.10 | async-start | bytes 4456448 | tf_op jit(solution)/shard_map/reduce_scatter | solution.py:273
  298.9 258.2 %reduce-scatter.5.cloned.1.call-start = ((), (), s32[]{:S(2)}) async-start(), calls=%async_computation.7 | async-start | bytes 4177920 | tf_op jit(solution)/shard_map/reduce_scatter | solution.py:273
  302.7 12.5 %collective-permute-start.5 = (bf16[512,512]{1,0:T(8,128)(2,1)S(1)}, bf16[512,512]{1,0:T(8,128)(2,1)S(1)}, u32[]{:S(2)}, u32[]{:S(2)}) collective-permute-start(bf16[512,512]{1,0:T(8,128)(2,1)S(1)} %get-tuple-element.105), channel_id=1, source_target_pairs={{0,16},{16,0},{1,17},{17,1},{2,18},{18,2},{3,19},{19,3},{4,20},{20... | collective-permute-start | bytes 1572872 | tf_op jit(solution)/shard_map/ppermute | solution.py:264
  374.3 26.1 %collective-permute-start.2 = (bf16[512,1024]{0,1:T(8,128)(2,1)S(1)}, bf16[512,1024]{0,1:T(8,128)(2,1)S(1)}, u32[]{:S(2)}, u32[]{:S(2)}) collective-permute-start(bf16[512,1024]{0,1:T(8,128)(2,1)S(1)} %slice.306), channel_id=1, source_target_pairs={{0,16},{16,0},{1,17},{17,1},{2,18},{18,2},{3,19},{19,3},{4,20},{20... | collective-permute-start | bytes 3145736 | tf_op jit(solution)/shard_map/ppermute | solution.py:264
  378.8 41.4 %collective-permute-start.6 = (bf16[512,1024]{0,1:T(8,128)(2,1)}, bf16[512,1024]{0,1:T(8,128)(2,1)S(1)}, u32[]{:S(2)}, u32[]{:S(2)}) collective-permute-start(bf16[512,1024]{0,1:T(8,128)(2,1)} %slice.304), channel_id=1, source_target_pairs={{0,16},{16,0},{1,17},{17,1},{2,18},{18,2},{3,19},{19,3},{4,20},{20... | collective-permute-start | bytes 3145736 | tf_op jit(solution)/shard_map/ppermute | solution.py:264
  403.9 81.3 %copy-start.13 = (bf16[1,512,1024]{1,2,0:T(8,128)(2,1)S(1)}, bf16[1,512,1024]{1,2,0:T(8,128)(2,1)}, u32[]{:S(2)}) copy-start(bf16[1,512,1024]{1,2,0:T(8,128)(2,1)} %copy-done.12) | copy-start | bytes 3145732
  403.9 81.3 %slice-start = ((f32[1024]{0:T(1024)}), f32[512]{0:T(512)S(1)}, s32[]{:S(2)}) async-start(f32[1024]{0:T(1024)} %copy-done.26), calls=%async_computation.12 | async-start | bytes 4096 | tf_op jit(solution)/shard_map/slice | solution.py:413
  423.2 70.1 %collective-permute-start.9 = (bf16[64,512]{1,0:T(8,128)(2,1)}, bf16[64,512]{1,0:T(8,128)(2,1)S(1)}, u32[]{:S(2)}, u32[]{:S(2)}) collective-permute-start(bf16[64,512]{1,0:T(8,128)(2,1)} %reduce-scatter.7.cloned.1.call-done), channel_id=1, source_target_pairs={{0,16},{16,0},{1,17},{17,1},{2,18},{18,2},{3,19},{19,3},{4,20},{20... | collective-permute-start | bytes 196616 | tf_op jit(solution)/shard_map/ppermute | solution.py:264
  424.7 69.4 %collective-permute-start.10 = (bf16[64,2048]{1,0:T(8,128)(2,1)}, bf16[64,2048]{1,0:T(8,128)(2,1)S(1)}, u32[]{:S(2)}, u32[]{:S(2)}) collective-permute-start(bf16[64,2048]{1,0:T(8,128)(2,1)} %reduce-scatter.9.cloned.1.call-done), channel_id=1, source_target_pairs={{0,16},{16,0},{1,17},{17,1},{2,18},{18,2},{3,19},{19,3},{4,20},{20... | collective-permute-start | bytes 786440 | tf_op jit(solution)/shard_map/ppermute | solution.py:264
  483.6 13.2 %collective-permute-start.11 = (bf16[128,1024]{1,0:T(8,128)(2,1)}, bf16[128,1024]{1,0:T(8,128)(2,1)}, u32[]{:S(2)}, u32[]{:S(2)}) collective-permute-start(bf16[128,1024]{1,0:T(8,128)(2,1)} %reduce-scatter.11.cloned.1.call-done), channel_id=1, source_target_pairs={{0,16},{16,0},{1,17},{17,1},{2,18},{18,2},{3,19},{19,3},{4,20},{20... | collective-permute-start | bytes 786440 | tf_op jit(solution)/shard_map/ppermute | solution.py:264
  557.1 6.5 %collective-permute-start.7 = (bf16[80,1536]{1,0:T(8,128)(2,1)}, bf16[80,1536]{1,0:T(8,128)(2,1)S(1)}, u32[]{:S(2)}, u32[]{:S(2)}) collective-permute-start(bf16[80,1536]{1,0:T(8,128)(2,1)} %reduce-scatter.5.cloned.1.call-done), channel_id=1, source_target_pairs={{0,16},{16,0},{1,17},{17,1},{2,18},{18,2},{3,19},{19,3},{4,20},{20... | collective-permute-start | bytes 737288 | tf_op jit(solution)/shard_map/ppermute | solution.py:264
  (27 other events, 479.1 us)
Sparse Core Ops, SparseCore 0:
  16.3 51.7 all-gather.5
  70.3 40.0 all-gather.7
  112.5 49.0 all-gather.9
  164.3 48.8 all-gather.11
  276.2 56.1 reduce-scatter.6
  336.1 71.8 reduce-scatter.8
  411.9 71.6 reduce-scatter.10
  487.5 69.5 reduce-scatter.4
